TPU v7x, 512 devices: a whole 4x8x8 slice. The times are simulated.
512 devices in a mesh: gx: 16 (over z, x_lo), gy: 8 (over y), gz: 4 (over x_hi, core).
Axes of the slice: x: 4 (x_hi: 2, x_lo: 2; x = x_hi * 2 + x_lo), y: 8, z: 8, core: 2. Of those that a mesh axis runs over, the one named last changes fastest.
Arguments:
- block_input: bfloat16 [64, 64, 4096], P('gx', 'gy', 'gz'), may hold values from -6 to 6
- pre_act: bfloat16 [64, 64, 4096], P('gx', 'gy', 'gz'), may hold values from -6 to 6
- skip_grad: bfloat16 [64, 64, 4096], P('gx', 'gy', 'gz'), may hold values from -6 to 6
- pool_grad: bfloat16 [32, 32, 2048], P('gx', 'gy', 'gz'), may hold values from -6 to 6
- conv1_weight: bfloat16 [64, 1728], P('gx'), may hold values from -0.15625 to 0.15625
- conv2_weight: bfloat16 [64, 1728], P('gx'), may hold values from -0.15625 to 0.15625
Outputs:
- input_grad: bfloat16 [64, 64, 4096], P('gx', 'gy', 'gz')
- conv1_grad: float32 [64, 1728], P('gx')
- conv2_grad: float32 [64, 1728], P('gx')
All inputs are finite; a program needn't handle non-finite values.
Results may differ from a plain program's by a relative error of at most 0.0053.
Values may be sent and summed in bfloat16 or wider, within the bound.
No kernel may reach another device: no remote copies, remote signals or barrier semaphores. Data moves between devices by JAX's collectives and lax.ppermute only.
A program may use at most 64 MiB of HBM per device.

v0:
```python
import math
import jax
import jax.numpy as jnp
from jax import lax
from jax.sharding import PartitionSpec as P


def padded_2(block, sides, width):
    for axis, dim in sides:
        count = lax.axis_size(axis)
        forward = [(i, i + 1) for i in range(count - 1)]
        forward.append((count - 1, 0))
        backward = [(target, source) for source, target in forward]
        low = lax.ppermute(
            lax.slice_in_dim(block, block.shape[dim] - width, None, axis=dim), axis, forward
        )
        high = lax.ppermute(lax.slice_in_dim(block, 0, width, axis=dim), axis, backward)
        block = jnp.concatenate([low, block, high], axis=dim)
    return block


def offset_of(k):
    return (k // 9 - 1, k // 3 % 3 - 1, k % 3 - 1)


def silu_slope(v):
    g = jax.nn.sigmoid(v)
    return g * (1.0 + v * (1.0 - g))


def window(padded, start, shape):
    lower = (start[0], start[1], start[2], 0)
    upper = (start[0] + shape[0], start[1] + shape[1], start[2] + shape[2], padded.shape[3])
    return lax.slice(padded, lower, upper).reshape(-1, padded.shape[3])


def transpose_conv(weight, padded, margin, shape):
    chans = weight.shape[0]
    total = None
    for k in range(27):
        d = offset_of(k)
        behind = window(padded, (margin - d[0], margin - d[1], margin - d[2]), shape)
        block = weight[:, k * chans : (k + 1) * chans]
        term = lax.dot_general(
            behind, block, (((1,), (0,)), ((), ())), preferred_element_type=jnp.float32
        )
        total = term if total is None else total + term
    return total


def weight_grad(left_flat, padded, margin, shape):
    pieces = []
    for k in range(27):
        d = offset_of(k)
        ahead = window(padded, (margin + d[0], margin + d[1], margin + d[2]), shape)
        pieces.append(
            lax.dot_general(
                left_flat, ahead, (((0,), (0,)), ((), ())), preferred_element_type=jnp.float32
            )
        )
    return jnp.concatenate(pieces, axis=1)


def body(block_input, pre_act, skip_grad, pool_grad, conv1_weight, conv2_weight):
    chans = conv1_weight.shape[1] // 27
    size_x, size_y, merged = block_input.shape
    size_z = merged // chans
    inner = (size_x, size_y, size_z)
    four_shape = (size_x, size_y, size_z, chans)
    weight_one, weight_two = (
        lax.all_gather(conv1_weight, "gx", axis=0, tiled=True),
        lax.all_gather(conv2_weight, "gx", axis=0, tiled=True),
    )
    pool_four = pool_grad.reshape(size_x // 2, size_y // 2, size_z // 2, chans).astype(jnp.float32)
    upsampled = jnp.repeat(jnp.repeat(jnp.repeat(pool_four, 2, axis=0), 2, axis=1), 2, axis=2)
    out_grad = (skip_grad.reshape(four_shape).astype(jnp.float32) + 0.125 * upsampled).astype(
        jnp.bfloat16
    )
    out_flat = out_grad.reshape(-1, chans)
    input_four = block_input.reshape(four_shape)
    pre_four = pre_act.reshape(four_shape)
    stacked = jnp.concatenate([input_four, pre_four, out_grad], axis=3)
    padded = padded_2(stacked, (("gx", 0), ("gy", 1), ("gz", 2)), 1)
    input_pad = padded[..., :chans]
    act_pad = jax.nn.silu(padded[..., chans : 2 * chans].astype(jnp.float32)).astype(jnp.bfloat16)
    grad_pad = padded[..., 2 * chans :]
    grads_two = weight_grad(out_flat, act_pad, 1, inner)
    act_grad = transpose_conv(weight_two, grad_pad, 1, inner)
    slope = silu_slope(pre_four.astype(jnp.float32)).reshape(-1, chans)
    pre_grad = (act_grad * slope).astype(jnp.bfloat16).reshape(four_shape)
    pre_pad = padded_2(pre_grad, (("gx", 0), ("gy", 1), ("gz", 2)), 1)
    pre_flat = pre_grad.reshape(-1, chans)
    grads_one = weight_grad(pre_flat, input_pad, 1, inner)
    total = out_grad.astype(jnp.float32).reshape(-1, chans) + transpose_conv(
        weight_one, pre_pad, 1, inner
    )
    input_grad = total.reshape(size_x, size_y, merged).astype(jnp.bfloat16)
    cells_all = (
        inner[0]
        * inner[1]
        * inner[2]
        * lax.axis_size("gx")
        * lax.axis_size("gy")
        * lax.axis_size("gz")
    )
    scale_all = 1.0 / math.sqrt(cells_all)
    grads_one = grads_one * scale_all
    grads_two = grads_two * scale_all
    owned = chans // lax.axis_size("gx")
    summed_one, summed_two = lax.psum((grads_one, grads_two), ("gx", "gy", "gz"))
    first = lax.axis_index("gx") * owned
    conv1_grad = lax.dynamic_slice_in_dim(summed_one, first, owned, 0)
    conv2_grad = lax.dynamic_slice_in_dim(summed_two, first, owned, 0)
    return (input_grad, conv1_grad, conv2_grad)


def solution(mesh):
    in_specs = (
        P("gx", "gy", "gz"),
        P("gx", "gy", "gz"),
        P("gx", "gy", "gz"),
        P("gx", "gy", "gz"),
        P("gx", None),
        P("gx", None),
    )
    out_specs = (P("gx", "gy", "gz"), P("gx", None), P("gx", None))
    return jax.shard_map(body, mesh=mesh, in_specs=in_specs, out_specs=out_specs, check_vma=False)
```

profile of v0, /device:TPU:1, one launch (start us, length us, event | category | flops | bytes accessed | tf_op | source)
XLA Modules:
  0.0 442.2 jit_solution(9441771854849640452)
XLA Ops:
  9.0 1.0 reshape.322
  10.0 1.0 reshape.321
  11.3 12.4 %collective-permute-start.1 = (bf16[1,8,16,192]{3,2,1,0:T(8,128)(2,1)S(1)}, bf16[1,8,16,192]{3,2,1,0:T(8,128)(2,1)S(1)}, u32[]{:S(2)}, u32[]{:S(2)}) collective-permute-start(bf16[1,8,16,192]{3,2,1,0:T(8,128)(2,1)S(1)} %get-tuple-element.68), channel_id=1, source_target_pairs={{32,0},{64,32},{96,64},{128,96},{160,128},{192,160},{224,192},{256... | collective-permute-start | bytes 147464 | tf_op jit(solution)/shard_map/ppermute | solution.py:17
  23.7 1.9 collective-permute-start
  26.1 27.4 %all-gather = bf16[16,4,1728]{2,1,0:T(4,128)(2,1)S(1)} all-gather(bf16[1,4,1728]{2,1,0:T(4,128)(2,1)S(1)} %bitcast.417), channel_id=1, replica_groups=mesh['gx'=16,'gy'=8,'gz'=4] {'gx'}, dimensions={0}, use_global_device_ids=true | all-gather | bytes 235008 | tf_op jit(solution)/shard_map/all_gather | solution.py:72
  54.9 24.1 %all-gather.1 = bf16[16,4,1728]{2,1,0:T(4,128)(2,1)S(1)} all-gather(bf16[1,4,1728]{2,1,0:T(4,128)(2,1)S(1)} %bitcast.418), channel_id=1, replica_groups=mesh['gx'=16,'gy'=8,'gz'=4] {'gx'}, dimensions={0}, use_global_device_ids=true | all-gather | bytes 235008 | tf_op jit(solution)/shard_map/all_gather | solution.py:71
  80.2 5.1 %collective-permute-start.3 = (bf16[6,1,16,192]{3,2,1,0:T(8,128)(2,1)S(1)}, bf16[6,1,16,192]{3,2,1,0:T(8,128)(2,1)S(1)}, u32[]{:S(2)}, u32[]{:S(2)}) collective-permute-start(bf16[6,1,16,192]{3,2,1,0:T(8,128)(2,1)S(1)} %get-tuple-element.48), channel_id=1, source_target_pairs={{4,0},{8,4},{12,8},{16,12},{20,16},{24,20},{28,24},{0,28},{5,1},{9... | collective-permute-start | bytes 110600 | tf_op jit(solution)/shard_map/ppermute | solution.py:17
  85.3 1.9 collective-permute-start.2
  88.2 3.5 collective-permute-done.2
  91.9 18.2 %collective-permute-start.4 = (bf16[6,10,1,192]{3,2,1,0:T(2,128)(2,1)S(1)}, bf16[6,10,1,192]{3,2,1,0:T(2,128)(2,1)S(1)}, u32[]{:S(2)}, u32[]{:S(2)}) collective-permute-start(bf16[6,10,1,192]{3,2,1,0:T(2,128)(2,1)S(1)} %get-tuple-element.43), channel_id=1, source_target_pairs={{1,0},{2,1},{3,2},{0,3},{5,4},{6,5},{7,6},{4,7},{9,8},{10,9},{11,1... | collective-permute-start | bytes 69128 | tf_op jit(solution)/shard_map/ppermute | solution.py:17
  110.1 4.3 collective-permute-start.5
  138.0 1.4 pad_maximum_fusion
  140.3 1.3 fusion.103
  148.1 2.9 collective-permute-start.7
  151.7 2.3 collective-permute-start.6
  154.7 1.1 fusion.116
  162.4 2.1 collective-permute-start.9
  164.5 3.4 collective-permute-start.8
  167.9 2.4 collective-permute-done.8
  170.3 5.3 %collective-permute-start.10 = (bf16[6,10,1,64]{3,2,1,0:T(2,128)(2,1)S(1)}, bf16[6,10,1,64]{3,2,1,0:T(2,128)(2,1)S(1)}, u32[]{:S(2)}, u32[]{:S(2)}) collective-permute-start(bf16[6,10,1,64]{3,2,1,0:T(2,128)(2,1)S(1)} %get-tuple-element.89), channel_id=1, source_target_pairs={{1,0},{2,1},{3,2},{0,3},{5,4},{6,5},{7,6},{4,7},{9,8},{10,9},{11,1... | collective-permute-start | bytes 23048 | tf_op jit(solution)/shard_map/ppermute | solution.py:17
  175.6 4.3 collective-permute-start.11
  188.4 244.0 %all-reduce.3.cloned.1.call-done = (f32[64,1728]{1,0:T(8,128)}, f32[64,1728]{1,0:T(8,128)}) async-done(((f32[64,1728]{1,0:T(8,128)}, f32[64,1728]{1,0:T(8,128)}), (f32[64,1728]{1,0:T(8,128)}, f32[64,1728]{1,0:T(8,128)})) %all-reduce.3.cloned.1.call-update) | async-done | bytes 884752 | tf_op jit(solution)/shard_map/psum | solution.py:110
  432.5 1.4 constant_dynamic-slice_fusion.1
  433.9 1.4 constant_dynamic-slice_fusion
  (239 shorter events, 53.0 us)
Async XLA Ops:
  7.2 425.3 %all-reduce.3.cloned.1.call-start = ((), (), s32[]{:S(2)}) async-start(), calls=%async_computation | async-start | bytes 1835008 | tf_op jit(solution)/shard_map/psum | solution.py:110
  11.0 14.6 %copy-start.5 = (bf16[4,8,1024]{2,1,0:T(8,128)(2,1)S(1)}, bf16[4,8,1024]{2,1,0:T(8,128)(2,1)}, u32[]{:S(2)}) copy-start(bf16[4,8,1024]{2,1,0:T(8,128)(2,1)} %param.8) | copy-start | bytes 196612
  11.3 14.8 %copy-start.36 = (bf16[4,1728]{1,0:T(4,128)(2,1)S(1)}, bf16[4,1728]{1,0:T(4,128)(2,1)}, u32[]{:S(2)}) copy-start(bf16[4,1728]{1,0:T(4,128)(2,1)} %param.11) | copy-start | bytes 41476
  11.3 68.8 %collective-permute-start.1 = (bf16[1,8,16,192]{3,2,1,0:T(8,128)(2,1)S(1)}, bf16[1,8,16,192]{3,2,1,0:T(8,128)(2,1)S(1)}, u32[]{:S(2)}, u32[]{:S(2)}) collective-permute-start(bf16[1,8,16,192]{3,2,1,0:T(8,128)(2,1)S(1)} %get-tuple-element.68), channel_id=1, source_target_pairs={{32,0},{64,32},{96,64},{128,96},{160,128},{192,160},{224,192},{256... | collective-permute-start | bytes 147464 | tf_op jit(solution)/shard_map/ppermute | solution.py:17
  23.7 56.4 %collective-permute-start = (bf16[1,8,16,192]{3,2,1,0:T(8,128)(2,1)S(1)}, bf16[1,8,16,192]{3,2,1,0:T(8,128)(2,1)S(1)}, u32[]{:S(2)}, u32[]{:S(2)}) collective-permute-start(bf16[1,8,16,192]{3,2,1,0:T(8,128)(2,1)S(1)} %get-tuple-element.67), channel_id=1, source_target_pairs={{0,32},{32,64},{64,96},{96,128},{128,160},{160,192},{192,224},{224... | collective-permute-start | bytes 147464 | tf_op jit(solution)/shard_map/ppermute | solution.py:14
  53.6 1.2 copy-start.37
  53.6 25.3 %copy-start.6 = (bf16[4,8,1024]{2,1,0:T(8,128)(2,1)S(1)}, bf16[4,8,1024]{2,1,0:T(8,128)(2,1)}, u32[]{:S(2)}) copy-start(bf16[4,8,1024]{2,1,0:T(8,128)(2,1)} %param.7) | copy-start | bytes 196612
  53.8 25.3 %copy-start.7 = (bf16[4,8,1024]{2,1,0:T(8,128)(2,1)S(1)}, bf16[4,8,1024]{2,1,0:T(8,128)(2,1)}, u32[]{:S(2)}) copy-start(bf16[4,8,1024]{2,1,0:T(8,128)(2,1)} %param.6) | copy-start | bytes 196612
  80.2 7.9 %collective-permute-start.3 = (bf16[6,1,16,192]{3,2,1,0:T(8,128)(2,1)S(1)}, bf16[6,1,16,192]{3,2,1,0:T(8,128)(2,1)S(1)}, u32[]{:S(2)}, u32[]{:S(2)}) collective-permute-start(bf16[6,1,16,192]{3,2,1,0:T(8,128)(2,1)S(1)} %get-tuple-element.48), channel_id=1, source_target_pairs={{4,0},{8,4},{12,8},{16,12},{20,16},{24,20},{28,24},{0,28},{5,1},{9... | collective-permute-start | bytes 110600 | tf_op jit(solution)/shard_map/ppermute | solution.py:17
  85.3 6.3 %collective-permute-start.2 = (bf16[6,1,16,192]{3,2,1,0:T(8,128)(2,1)S(1)}, bf16[6,1,16,192]{3,2,1,0:T(8,128)(2,1)S(1)}, u32[]{:S(2)}, u32[]{:S(2)}) collective-permute-start(bf16[6,1,16,192]{3,2,1,0:T(8,128)(2,1)S(1)} %get-tuple-element.47), channel_id=1, source_target_pairs={{0,4},{4,8},{8,12},{12,16},{16,20},{20,24},{24,28},{28,0},{1,5},{5... | collective-permute-start | bytes 110600 | tf_op jit(solution)/shard_map/ppermute | solution.py:14
  91.9 23.3 %collective-permute-start.4 = (bf16[6,10,1,192]{3,2,1,0:T(2,128)(2,1)S(1)}, bf16[6,10,1,192]{3,2,1,0:T(2,128)(2,1)S(1)}, u32[]{:S(2)}, u32[]{:S(2)}) collective-permute-start(bf16[6,10,1,192]{3,2,1,0:T(2,128)(2,1)S(1)} %get-tuple-element.43), channel_id=1, source_target_pairs={{1,0},{2,1},{3,2},{0,3},{5,4},{6,5},{7,6},{4,7},{9,8},{10,9},{11,1... | collective-permute-start | bytes 69128 | tf_op jit(solution)/shard_map/ppermute | solution.py:17
  110.1 5.5 %collective-permute-start.5 = (bf16[6,10,1,192]{3,2,1,0:T(2,128)(2,1)S(1)}, bf16[6,10,1,192]{3,2,1,0:T(2,128)(2,1)S(1)}, u32[]{:S(2)}, u32[]{:S(2)}) collective-permute-start(bf16[6,10,1,192]{3,2,1,0:T(2,128)(2,1)S(1)} %get-tuple-element.44), channel_id=1, source_target_pairs={{0,1},{1,2},{2,3},{3,0},{4,5},{5,6},{6,7},{7,4},{8,9},{9,10},{10,1... | collective-permute-start | bytes 69128 | tf_op jit(solution)/shard_map/ppermute | solution.py:14
  147.3 8.4 %copy-start.2 = (bf16[4,8,16,64]{3,2,1,0:T(8,128)(2,1)S(1)}, bf16[4,8,16,64]{3,2,1,0:T(8,128)(2,1)}, u32[]{:S(2)}) copy-start(bf16[4,8,16,64]{3,2,1,0:T(8,128)(2,1)} %get-tuple-element.12) | copy-start | bytes 196612
  148.1 14.2 %collective-permute-start.7 = (bf16[1,8,16,64]{3,2,1,0:T(8,128)(2,1)}, bf16[1,8,16,64]{3,2,1,0:T(8,128)(2,1)S(1)}, u32[]{:S(2)}, u32[]{:S(2)}) collective-permute-start(bf16[1,8,16,64]{3,2,1,0:T(8,128)(2,1)} %bitcast.33), channel_id=1, source_target_pairs={{32,0},{64,32},{96,64},{128,96},{160,128},{192,160},{224,192},{256... | collective-permute-start | bytes 49160 | tf_op jit(solution)/shard_map/ppermute | solution.py:17
  151.7 10.6 %collective-permute-start.6 = (bf16[1,8,16,64]{3,2,1,0:T(8,128)(2,1)}, bf16[1,8,16,64]{3,2,1,0:T(8,128)(2,1)S(1)}, u32[]{:S(2)}, u32[]{:S(2)}) collective-permute-start(bf16[1,8,16,64]{3,2,1,0:T(8,128)(2,1)} %bitcast.31), channel_id=1, source_target_pairs={{0,32},{32,64},{64,96},{96,128},{128,160},{160,192},{192,224},{224... | collective-permute-start | bytes 49160 | tf_op jit(solution)/shard_map/ppermute | solution.py:14
  154.4 1.9 copy-start.1
  159.5 1.1 copy-start.9
  159.5 1.1 copy-start.10
  159.5 1.1 copy-start.11
  159.5 1.1 copy-start.12
  162.4 5.5 %collective-permute-start.9 = (bf16[6,1,16,64]{3,2,1,0:T(8,128)(2,1)S(1)}, bf16[6,1,16,64]{3,2,1,0:T(8,128)(2,1)S(1)}, u32[]{:S(2)}, u32[]{:S(2)}) collective-permute-start(bf16[6,1,16,64]{3,2,1,0:T(8,128)(2,1)S(1)} %get-tuple-element.100), channel_id=1, source_target_pairs={{4,0},{8,4},{12,8},{16,12},{20,16},{24,20},{28,24},{0,28},{5,1},{9... | collective-permute-start | bytes 36872 | tf_op jit(solution)/shard_map/ppermute | solution.py:17
  164.5 5.8 %collective-permute-start.8 = (bf16[6,1,16,64]{3,2,1,0:T(8,128)(2,1)S(1)}, bf16[6,1,16,64]{3,2,1,0:T(8,128)(2,1)S(1)}, u32[]{:S(2)}, u32[]{:S(2)}) collective-permute-start(bf16[6,1,16,64]{3,2,1,0:T(8,128)(2,1)S(1)} %get-tuple-element.99), channel_id=1, source_target_pairs={{0,4},{4,8},{8,12},{12,16},{16,20},{20,24},{24,28},{28,0},{1,5},{5... | collective-permute-start | bytes 36872 | tf_op jit(solution)/shard_map/ppermute | solution.py:14
  170.3 10.0 %collective-permute-start.10 = (bf16[6,10,1,64]{3,2,1,0:T(2,128)(2,1)S(1)}, bf16[6,10,1,64]{3,2,1,0:T(2,128)(2,1)S(1)}, u32[]{:S(2)}, u32[]{:S(2)}) collective-permute-start(bf16[6,10,1,64]{3,2,1,0:T(2,128)(2,1)S(1)} %get-tuple-element.89), channel_id=1, source_target_pairs={{1,0},{2,1},{3,2},{0,3},{5,4},{6,5},{7,6},{4,7},{9,8},{10,9},{11,1... | collective-permute-start | bytes 23048 | tf_op jit(solution)/shard_map/ppermute | solution.py:17
  175.6 5.2 %collective-permute-start.11 = (bf16[6,10,1,64]{3,2,1,0:T(2,128)(2,1)S(1)}, bf16[6,10,1,64]{3,2,1,0:T(2,128)(2,1)S(1)}, u32[]{:S(2)}, u32[]{:S(2)}) collective-permute-start(bf16[6,10,1,64]{3,2,1,0:T(2,128)(2,1)S(1)} %get-tuple-element.90), channel_id=1, source_target_pairs={{0,1},{1,2},{2,3},{3,0},{4,5},{5,6},{6,7},{7,4},{8,9},{9,10},{10,1... | collective-permute-start | bytes 23048 | tf_op jit(solution)/shard_map/ppermute | solution.py:14
  (27 other events, 28.4 us)
Sparse Core Ops, SparseCore 0:
  162.4 269.9 all-reduce.2
where the time goes:
time: 443 us; the launch traced here: 442 us
  waiting for transfers between devices  251 us (57%)
  starting transfers between devices  64.1 us (14%)
  blocking collectives  51.5 us (12%)
  matrix products  40.7 us (9%)
  between operations  15 us (3%)
  local copies, waits for them, and re-layouts  13.2 us (3%)
  other arithmetic  6.58 us (1%)
    psum x1, waiting for transfers between devices, body(): lax.psum((grads_one, grads_two), ('gx', 'gy', 'gz'))  244 us
    ppermute x6, starting transfers between devices, padded_2(): lax.ppermute(lax.slice_in_dim(block, 0, width, axis=dim), axis, backward)  46.1 us
    all_gather x1, blocking collectives, body(): lax.all_gather(conv2_weight, 'gx', axis=0, tiled=True)  27.4 us
    dot_general x54, matrix products, weight_grad(): lax.dot_general(left_flat, ahead, (((0,), (0,)), ((), ())), preferred_ele...  26.9 us
    all_gather x1, blocking collectives, body(): lax.all_gather(conv1_weight, 'gx', axis=0, tiled=True)  24.1 us
    ppermute x6, starting transfers between devices, padded_2(): lax.ppermute(lax.slice_in_dim(block, block.shape[dim] - width, None, axis...  18.1 us
    dot_general x54, matrix products, transpose_conv(): lax.dot_general(behind, block, (((1,), (0,)), ((), ())), preferred_elemen...  13.8 us
  transfers between devices with their start and end apart: 13, of which 5 were waited for; matrix products, arithmetic and copies ran while one was open for 5% of the time, Pallas kernels for 0%

commit v1 on v0

--- a/solution.py
+++ b/solution.py
@@ -68,7 +68,9 @@
     inner = (size_x, size_y, size_z)
     four_shape = (size_x, size_y, size_z, chans)
     weight_one, weight_two = (
-        lax.all_gather(conv1_weight, "gx", axis=0, tiled=True),
+        jnp.concatenate(
+            lax.all_to_all(jnp.stack([conv1_weight] * lax.axis_size("gx")), "gx", 0, 0), axis=0
+        ),
         lax.all_gather(conv2_weight, "gx", axis=0, tiled=True),
     )
     pool_four = pool_grad.reshape(size_x // 2, size_y // 2, size_z // 2, chans).astype(jnp.float32)

time: 443 us -> 421 us (0.950)
  blocking collectives: 51.5 us -> 27.7 us
    all_gather x1 -> x0, blocking collectives: 24.1 us -> none  [body(): lax.all_gather(conv1_weight, 'gx', axis=0, tiled=True)]
    ppermute x6, starting transfers between devices: 46.1 us -> 38.7 us  [padded_2(): lax.ppermute(lax.slice_in_dim(block, 0, width, axis=dim), axis, backward)]
    all_to_all x0 -> x1, starting transfers between devices: none -> 4.94 us  [body(): lax.all_to_all(jnp.stack([conv1_weight] * lax.axis_size('gx')), 'gx', 0, 0)]
  transfers between devices with their start and end apart: 13 -> 14, of which waited for: 5 -> 4; matrix products, arithmetic and copies ran while one was open for 5% -> 14% of each run, Pallas kernels for 0% -> 0%
where the time goes in v1:
time: 421 us; the launch traced here: 420 us
  waiting for transfers between devices  248 us (59%)
  starting transfers between devices  62.9 us (15%)
  matrix products  41.5 us (10%)
  blocking collectives  27.7 us (7%)
  local copies, waits for them, and re-layouts  17.2 us (4%)
  between operations  15 us (4%)
  other arithmetic  7.28 us (2%)
    psum x1, waiting for transfers between devices, body(): lax.psum((grads_one, grads_two), ('gx', 'gy', 'gz'))  243 us
    ppermute x6, starting transfers between devices, padded_2(): lax.ppermute(lax.slice_in_dim(block, 0, width, axis=dim), axis, backward)  38.7 us
    dot_general x54, matrix products, weight_grad(): lax.dot_general(left_flat, ahead, (((0,), (0,)), ((), ())), preferred_ele...  27.8 us
    all_gather x1, blocking collectives, body(): lax.all_gather(conv2_weight, 'gx', axis=0, tiled=True)  27.7 us
    ppermute x6, starting transfers between devices, padded_2(): lax.ppermute(lax.slice_in_dim(block, block.shape[dim] - width, None, axis...  19.2 us
    dot_general x54, matrix products, transpose_conv(): lax.dot_general(behind, block, (((1,), (0,)), ((), ())), preferred_elemen...  13.8 us
  transfers between devices with their start and end apart: 14, of which 4 were waited for; matrix products, arithmetic and copies ran while one was open for 14% of the time, Pallas kernels for 0%

profile of v1, /device:TPU:1, one launch (start us, length us, event | category | flops | bytes accessed | tf_op | source)
XLA Modules:
  0.0 419.7 jit_solution(6956273285536803984)
XLA Ops:
  8.9 1.0 reshape.327
  9.9 1.0 reshape.326
  11.3 12.4 %collective-permute-start.1 = (bf16[1,8,16,192]{3,2,1,0:T(8,128)(2,1)S(1)}, bf16[1,8,16,192]{3,2,1,0:T(8,128)(2,1)S(1)}, u32[]{:S(2)}, u32[]{:S(2)}) collective-permute-start(bf16[1,8,16,192]{3,2,1,0:T(8,128)(2,1)S(1)} %get-tuple-element.68), channel_id=1, source_target_pairs={{32,0},{64,32},{96,64},{128,96},{160,128},{192,160},{224,192},{256... | collective-permute-start | bytes 147464 | tf_op jit(solution)/shard_map/ppermute | solution.py:17
  23.7 1.9 collective-permute-start
  26.4 4.9 %all-to-all-start = ((bf16[16,4,1728]{2,1,0:T(4,128)(2,1)}), bf16[16,4,1728]{2,1,0:T(4,128)(2,1)S(1)}, u32[]{:S(2)}, u32[]{:S(2)}) async-start(bf16[16,4,1728]{2,1,0:T(4,128)(2,1)} %stack.2), calls=%async_computation | async-start | bytes 458752 | tf_op jit(solution)/shard_map/all_to_all | solution.py:72
  31.5 27.7 %all-gather = bf16[16,4,1728]{2,1,0:T(4,128)(2,1)S(1)} all-gather(bf16[1,4,1728]{2,1,0:T(4,128)(2,1)S(1)} %bitcast.416), channel_id=1, replica_groups=mesh['gx'=16,'gy'=8,'gz'=4] {'gx'}, dimensions={0}, use_global_device_ids=true | all-gather | bytes 235008 | tf_op jit(solution)/shard_map/all_gather | solution.py:74
  62.4 5.1 %collective-permute-start.3 = (bf16[6,1,16,192]{3,2,1,0:T(8,128)(2,1)S(1)}, bf16[6,1,16,192]{3,2,1,0:T(8,128)(2,1)S(1)}, u32[]{:S(2)}, u32[]{:S(2)}) collective-permute-start(bf16[6,1,16,192]{3,2,1,0:T(8,128)(2,1)S(1)} %get-tuple-element.48), channel_id=1, source_target_pairs={{4,0},{8,4},{12,8},{16,12},{20,16},{24,20},{28,24},{0,28},{5,1},{9... | collective-permute-start | bytes 110600 | tf_op jit(solution)/shard_map/ppermute | solution.py:17
  67.5 1.9 collective-permute-start.2
  70.3 3.2 collective-permute-done.2
  73.8 12.1 %collective-permute-start.4 = (bf16[6,10,1,192]{3,2,1,0:T(2,128)(2,1)S(1)}, bf16[6,10,1,192]{3,2,1,0:T(2,128)(2,1)S(1)}, u32[]{:S(2)}, u32[]{:S(2)}) collective-permute-start(bf16[6,10,1,192]{3,2,1,0:T(2,128)(2,1)S(1)} %get-tuple-element.43), channel_id=1, source_target_pairs={{1,0},{2,1},{3,2},{0,3},{5,4},{6,5},{7,6},{4,7},{9,8},{10,9},{11,1... | collective-permute-start | bytes 69128 | tf_op jit(solution)/shard_map/ppermute | solution.py:17
  85.9 4.3 %collective-permute-start.5 = (bf16[6,10,1,192]{3,2,1,0:T(2,128)(2,1)S(1)}, bf16[6,10,1,192]{3,2,1,0:T(2,128)(2,1)S(1)}, u32[]{:S(2)}, u32[]{:S(2)}) collective-permute-start(bf16[6,10,1,192]{3,2,1,0:T(2,128)(2,1)S(1)} %get-tuple-element.44), channel_id=1, source_target_pairs={{0,1},{1,2},{2,3},{3,0},{4,5},{5,6},{6,7},{7,4},{8,9},{9,10},{10,1... | collective-permute-start | bytes 69128 | tf_op jit(solution)/shard_map/ppermute | solution.py:14
  113.9 1.4 pad_maximum_fusion
  116.3 1.3 fusion.103
  124.0 1.9 collective-permute-start.7
  126.6 3.5 collective-permute-start.6
  131.4 1.1 fusion.116
  138.8 1.9 collective-permute-start.9
  140.8 3.4 collective-permute-start.8
  144.8 1.7 collective-permute-done.8
  146.6 5.3 %collective-permute-start.10 = (bf16[6,10,1,64]{3,2,1,0:T(2,128)(2,1)S(1)}, bf16[6,10,1,64]{3,2,1,0:T(2,128)(2,1)S(1)}, u32[]{:S(2)}, u32[]{:S(2)}) collective-permute-start(bf16[6,10,1,64]{3,2,1,0:T(2,128)(2,1)S(1)} %get-tuple-element.89), channel_id=1, source_target_pairs={{1,0},{2,1},{3,2},{0,3},{5,4},{6,5},{7,6},{4,7},{9,8},{10,9},{11,1... | collective-permute-start | bytes 23048 | tf_op jit(solution)/shard_map/ppermute | solution.py:17
  151.9 4.3 %collective-permute-start.11 = (bf16[6,10,1,64]{3,2,1,0:T(2,128)(2,1)S(1)}, bf16[6,10,1,64]{3,2,1,0:T(2,128)(2,1)S(1)}, u32[]{:S(2)}, u32[]{:S(2)}) collective-permute-start(bf16[6,10,1,64]{3,2,1,0:T(2,128)(2,1)S(1)} %get-tuple-element.90), channel_id=1, source_target_pairs={{0,1},{1,2},{2,3},{3,0},{4,5},{5,6},{6,7},{7,4},{8,9},{9,10},{10,1... | collective-permute-start | bytes 23048 | tf_op jit(solution)/shard_map/ppermute | solution.py:14
  167.4 242.7 %all-reduce.3.cloned.1.call-done = (f32[64,1728]{1,0:T(8,128)}, f32[64,1728]{1,0:T(8,128)}) async-done(((f32[64,1728]{1,0:T(8,128)}, f32[64,1728]{1,0:T(8,128)}), (f32[64,1728]{1,0:T(8,128)}, f32[64,1728]{1,0:T(8,128)})) %all-reduce.3.cloned.1.call-update) | async-done | bytes 884752 | tf_op jit(solution)/shard_map/psum | solution.py:112
  410.0 1.4 constant_dynamic-slice_fusion.1
  411.5 1.4 constant_dynamic-slice_fusion
  (259 shorter events, 57.9 us)
Async XLA Ops:
  11.0 14.7 %copy-start.45 = (bf16[4,1728]{1,0:T(4,128)(2,1)S(1)}, bf16[4,1728]{1,0:T(4,128)(2,1)}, u32[]{:S(2)}) copy-start(bf16[4,1728]{1,0:T(4,128)(2,1)} %param.10) | copy-start | bytes 41476
  11.1 20.3 %copy-start.13 = (bf16[4,8,1024]{2,1,0:T(8,128)(2,1)S(1)}, bf16[4,8,1024]{2,1,0:T(8,128)(2,1)}, u32[]{:S(2)}) copy-start(bf16[4,8,1024]{2,1,0:T(8,128)(2,1)} %param.8) | copy-start | bytes 196612
  11.1 20.4 %copy-start.46 = (bf16[4,1728]{1,0:T(4,128)(2,1)S(1)}, bf16[4,1728]{1,0:T(4,128)(2,1)}, u32[]{:S(2)}) copy-start(bf16[4,1728]{1,0:T(4,128)(2,1)} %param.11) | copy-start | bytes 41476
  11.3 51.0 %collective-permute-start.1 = (bf16[1,8,16,192]{3,2,1,0:T(8,128)(2,1)S(1)}, bf16[1,8,16,192]{3,2,1,0:T(8,128)(2,1)S(1)}, u32[]{:S(2)}, u32[]{:S(2)}) collective-permute-start(bf16[1,8,16,192]{3,2,1,0:T(8,128)(2,1)S(1)} %get-tuple-element.68), channel_id=1, source_target_pairs={{32,0},{64,32},{96,64},{128,96},{160,128},{192,160},{224,192},{256... | collective-permute-start | bytes 147464 | tf_op jit(solution)/shard_map/ppermute | solution.py:17
  23.7 38.6 %collective-permute-start = (bf16[1,8,16,192]{3,2,1,0:T(8,128)(2,1)S(1)}, bf16[1,8,16,192]{3,2,1,0:T(8,128)(2,1)S(1)}, u32[]{:S(2)}, u32[]{:S(2)}) collective-permute-start(bf16[1,8,16,192]{3,2,1,0:T(8,128)(2,1)S(1)} %get-tuple-element.67), channel_id=1, source_target_pairs={{0,32},{32,64},{64,96},{96,128},{128,160},{160,192},{192,224},{224... | collective-permute-start | bytes 147464 | tf_op jit(solution)/shard_map/ppermute | solution.py:14
  26.4 132.7 %all-to-all-start = ((bf16[16,4,1728]{2,1,0:T(4,128)(2,1)}), bf16[16,4,1728]{2,1,0:T(4,128)(2,1)S(1)}, u32[]{:S(2)}, u32[]{:S(2)}) async-start(bf16[16,4,1728]{2,1,0:T(4,128)(2,1)} %stack.2), calls=%async_computation | async-start | bytes 458752 | tf_op jit(solution)/shard_map/all_to_all | solution.py:72
  31.3 378.7 %all-reduce.3.cloned.1.call-start = ((), (), s32[]{:S(2)}) async-start(), calls=%async_computation.1 | async-start | bytes 1835008 | tf_op jit(solution)/shard_map/psum | solution.py:112
  59.6 1.3 copy-start.14
  62.4 7.9 %collective-permute-start.3 = (bf16[6,1,16,192]{3,2,1,0:T(8,128)(2,1)S(1)}, bf16[6,1,16,192]{3,2,1,0:T(8,128)(2,1)S(1)}, u32[]{:S(2)}, u32[]{:S(2)}) collective-permute-start(bf16[6,1,16,192]{3,2,1,0:T(8,128)(2,1)S(1)} %get-tuple-element.48), channel_id=1, source_target_pairs={{4,0},{8,4},{12,8},{16,12},{20,16},{24,20},{28,24},{0,28},{5,1},{9... | collective-permute-start | bytes 110600 | tf_op jit(solution)/shard_map/ppermute | solution.py:17
  67.5 6.0 %collective-permute-start.2 = (bf16[6,1,16,192]{3,2,1,0:T(8,128)(2,1)S(1)}, bf16[6,1,16,192]{3,2,1,0:T(8,128)(2,1)S(1)}, u32[]{:S(2)}, u32[]{:S(2)}) collective-permute-start(bf16[6,1,16,192]{3,2,1,0:T(8,128)(2,1)S(1)} %get-tuple-element.47), channel_id=1, source_target_pairs={{0,4},{4,8},{8,12},{12,16},{16,20},{20,24},{24,28},{28,0},{1,5},{5... | collective-permute-start | bytes 110600 | tf_op jit(solution)/shard_map/ppermute | solution.py:14
  73.8 17.2 %collective-permute-start.4 = (bf16[6,10,1,192]{3,2,1,0:T(2,128)(2,1)S(1)}, bf16[6,10,1,192]{3,2,1,0:T(2,128)(2,1)S(1)}, u32[]{:S(2)}, u32[]{:S(2)}) collective-permute-start(bf16[6,10,1,192]{3,2,1,0:T(2,128)(2,1)S(1)} %get-tuple-element.43), channel_id=1, source_target_pairs={{1,0},{2,1},{3,2},{0,3},{5,4},{6,5},{7,6},{4,7},{9,8},{10,9},{11,1... | collective-permute-start | bytes 69128 | tf_op jit(solution)/shard_map/ppermute | solution.py:17
  85.9 5.5 %collective-permute-start.5 = (bf16[6,10,1,192]{3,2,1,0:T(2,128)(2,1)S(1)}, bf16[6,10,1,192]{3,2,1,0:T(2,128)(2,1)S(1)}, u32[]{:S(2)}, u32[]{:S(2)}) collective-permute-start(bf16[6,10,1,192]{3,2,1,0:T(2,128)(2,1)S(1)} %get-tuple-element.44), channel_id=1, source_target_pairs={{0,1},{1,2},{2,3},{3,0},{4,5},{5,6},{6,7},{7,4},{8,9},{9,10},{10,1... | collective-permute-start | bytes 69128 | tf_op jit(solution)/shard_map/ppermute | solution.py:14
  123.2 9.2 %copy-start.2 = (bf16[4,8,16,64]{3,2,1,0:T(8,128)(2,1)S(1)}, bf16[4,8,16,64]{3,2,1,0:T(8,128)(2,1)}, u32[]{:S(2)}) copy-start(bf16[4,8,16,64]{3,2,1,0:T(8,128)(2,1)} %get-tuple-element.12) | copy-start | bytes 196612
  124.0 14.8 %collective-permute-start.7 = (bf16[1,8,16,64]{3,2,1,0:T(8,128)(2,1)}, bf16[1,8,16,64]{3,2,1,0:T(8,128)(2,1)S(1)}, u32[]{:S(2)}, u32[]{:S(2)}) collective-permute-start(bf16[1,8,16,64]{3,2,1,0:T(8,128)(2,1)} %bitcast.33), channel_id=1, source_target_pairs={{32,0},{64,32},{96,64},{128,96},{160,128},{192,160},{224,192},{256... | collective-permute-start | bytes 49160 | tf_op jit(solution)/shard_map/ppermute | solution.py:17
  126.6 12.2 %collective-permute-start.6 = (bf16[1,8,16,64]{3,2,1,0:T(8,128)(2,1)}, bf16[1,8,16,64]{3,2,1,0:T(8,128)(2,1)S(1)}, u32[]{:S(2)}, u32[]{:S(2)}) collective-permute-start(bf16[1,8,16,64]{3,2,1,0:T(8,128)(2,1)} %bitcast.31), channel_id=1, source_target_pairs={{0,32},{32,64},{64,96},{96,128},{128,160},{160,192},{192,224},{224... | collective-permute-start | bytes 49160 | tf_op jit(solution)/shard_map/ppermute | solution.py:14
  130.5 2.5 copy-start.1
  136.2 1.1 copy-start.18
  136.2 1.1 copy-start.19
  138.8 6.0 %collective-permute-start.9 = (bf16[6,1,16,64]{3,2,1,0:T(8,128)(2,1)S(1)}, bf16[6,1,16,64]{3,2,1,0:T(8,128)(2,1)S(1)}, u32[]{:S(2)}, u32[]{:S(2)}) collective-permute-start(bf16[6,1,16,64]{3,2,1,0:T(8,128)(2,1)S(1)} %get-tuple-element.100), channel_id=1, source_target_pairs={{4,0},{8,4},{12,8},{16,12},{20,16},{24,20},{28,24},{0,28},{5,1},{9... | collective-permute-start | bytes 36872 | tf_op jit(solution)/shard_map/ppermute | solution.py:17
  140.8 5.8 %collective-permute-start.8 = (bf16[6,1,16,64]{3,2,1,0:T(8,128)(2,1)S(1)}, bf16[6,1,16,64]{3,2,1,0:T(8,128)(2,1)S(1)}, u32[]{:S(2)}, u32[]{:S(2)}) collective-permute-start(bf16[6,1,16,64]{3,2,1,0:T(8,128)(2,1)S(1)} %get-tuple-element.99), channel_id=1, source_target_pairs={{0,4},{4,8},{8,12},{12,16},{16,20},{20,24},{24,28},{28,0},{1,5},{5... | collective-permute-start | bytes 36872 | tf_op jit(solution)/shard_map/ppermute | solution.py:14
  146.6 11.2 %collective-permute-start.10 = (bf16[6,10,1,64]{3,2,1,0:T(2,128)(2,1)S(1)}, bf16[6,10,1,64]{3,2,1,0:T(2,128)(2,1)S(1)}, u32[]{:S(2)}, u32[]{:S(2)}) collective-permute-start(bf16[6,10,1,64]{3,2,1,0:T(2,128)(2,1)S(1)} %get-tuple-element.89), channel_id=1, source_target_pairs={{1,0},{2,1},{3,2},{0,3},{5,4},{6,5},{7,6},{4,7},{9,8},{10,9},{11,1... | collective-permute-start | bytes 23048 | tf_op jit(solution)/shard_map/ppermute | solution.py:17
  151.9 6.0 %collective-permute-start.11 = (bf16[6,10,1,64]{3,2,1,0:T(2,128)(2,1)S(1)}, bf16[6,10,1,64]{3,2,1,0:T(2,128)(2,1)S(1)}, u32[]{:S(2)}, u32[]{:S(2)}) collective-permute-start(bf16[6,10,1,64]{3,2,1,0:T(2,128)(2,1)S(1)} %get-tuple-element.90), channel_id=1, source_target_pairs={{0,1},{1,2},{2,3},{3,0},{4,5},{5,6},{6,7},{7,4},{8,9},{9,10},{10,1... | collective-permute-start | bytes 23048 | tf_op jit(solution)/shard_map/ppermute | solution.py:14
  161.3 1.2 copy-start.7
  163.4 1.2 copy-start.4
  (37 other events, 38.7 us)
Sparse Core Ops, SparseCore 0:
  138.9 271.0 all-reduce.2
